TPU v7x, 32 devices: a whole 2x2x4 slice. The times are simulated.
32 devices in a mesh: groups: 2 (over y), seq: 4 (over x, core), role: 4 (over z).
Axes of the slice: x: 2, y: 2, z: 4, core: 2. Of those that a mesh axis runs over, the one named last changes fastest.
Arguments:
- query_rows: bfloat16 [8, 256, 4096], P('groups', 'seq', 'role'), parts along dimension 0, may hold values from -6 to 6
- encoded_key_rows: bfloat16 [8, 256, 512], P('groups', ('seq', 'role')), parts along dimension 0, may hold values from -6 to 6
- value_matrix_rows: bfloat16 [8, 256, 512], P('groups', ('seq', 'role')), parts along dimension 0, may hold values from -6 to 6
- output_weight: bfloat16 [4096, 2048], P('role', 'seq'), may hold values from -0.09375 to 0.09375
- residual: bfloat16 [8, 256, 2048], P(('groups', 'role'), 'seq'), parts along dimension 0, may hold values from -7.5 to 7.5
- norm_gain: float32 [2048], replicated, may hold values from 0.5 to 1.5
- route_experts: int32 [8, 256, 8], P(('groups', 'role'), 'seq'), parts along dimension 0, may hold values from 0 to 15, all different within a row; in each aligned block of 64 rows (0 to 63, 64 to 127, ..., all dimensions but the last counted through in order) at most 33 rows name the same one
- route_gates: float32 [8, 256, 8], P(('groups', 'role'), 'seq'), parts along dimension 0, may hold values from 0.05 to 0.3
- gate_weight: bfloat16 [16, 2048, 768], P(('seq', 'role')), may hold values from -0.125 to 0.125
- up_weight: bfloat16 [16, 2048, 768], P(('seq', 'role')), may hold values from -0.125 to 0.125
- down_weight: bfloat16 [16, 768, 2048], P(('seq', 'role')), may hold values from -0.21875 to 0.21875
Outputs:
- layer_output: bfloat16 [8, 256, 2048], P(('groups', 'role'), 'seq'), parts along dimension 0
There are 2 independent parts, one for each index of `groups`. A program takes and returns all parts, laid end to end along the dimension named above; an argument that names none is the same for every part. Nothing has to cross between parts.
Inputs may be any that keep to these rules, and one draw needn't show every extreme that they name: `route_experts`: each token names 8 different experts. Within the 64 positions of one sequence that one index of seq holds, no expert is named by more than 33 routes, and in every draw some expert is named by exactly 33 routes in some such block.
All inputs are finite; a program needn't handle non-finite values.
Results may differ from a plain program's by a relative error of at most 0.014.
Values may be sent and summed in bfloat16 or wider, within the bound.
A program may use at most 128 MiB of HBM per device.

v0:
```python
from functools import partial

import jax
import jax.numpy as jnp
from jax import lax
from jax.sharding import PartitionSpec as P

D = 2048
QUERY_HEADS = 32
KEY_VALUE_HEADS = 4
HEAD_WIDTH = 128
TOPK = 8


epsilon = 1e-06
masked_score = -1e30


def score_block(queries, every_key, query_position, block_start, block_width, score_scale):
    keys_part = lax.slice_in_dim(every_key, block_start, block_start + block_width, axis=0)
    raw_scores = (
        jnp.einsum("qhd,kd->hqk", queries, keys_part, preferred_element_type=jnp.float32)
        * score_scale
    )
    key_position = block_start + jnp.arange(block_width, dtype=jnp.int32)
    return jnp.where(
        key_position[None, None, :] <= query_position[None, :, None], raw_scores, masked_score
    )


def value_block(rounded, every_value, block_start, block_width):
    prob_block = lax.slice_in_dim(rounded, block_start, block_start + block_width, axis=2)
    values_part = lax.slice_in_dim(every_value, block_start, block_start + block_width, axis=0)
    return jnp.einsum("hqk,kd->qhd", prob_block, values_part, preferred_element_type=jnp.float32)


def shards(
    query_rows,
    encoded_key_rows,
    value_matrix_rows,
    output_weight,
    residual,
    norm_gain,
    route_experts,
    route_gates,
    gate_weight,
    up_weight,
    down_weight,
):
    seq_count = lax.axis_size("seq")
    role_count = lax.axis_size("role")
    seq_index = lax.axis_index("seq")
    role_index = lax.axis_index("role")
    batch_count = query_rows.shape[0]
    local_length = query_rows.shape[1]
    local_heads = query_rows.shape[2] // HEAD_WIDTH
    full_length = local_length * seq_count
    query_group_width = QUERY_HEADS // KEY_VALUE_HEADS
    head_pick = role_index * local_heads // query_group_width
    role_keys, role_values = (
        lax.all_gather(encoded_key_rows, "role", axis=1, tiled=True),
        lax.all_gather(value_matrix_rows, "role", axis=1, tiled=True),
    )
    head_keys = lax.dynamic_slice_in_dim(role_keys, head_pick * HEAD_WIDTH, HEAD_WIDTH, 2)
    head_values = lax.dynamic_slice_in_dim(role_values, head_pick * HEAD_WIDTH, HEAD_WIDTH, 2)
    whole_keys, whole_values, whole_proj = (
        lax.all_gather(head_keys, "seq", axis=1, tiled=True),
        lax.all_gather(head_values, "seq", axis=1, tiled=True),
        lax.all_gather(output_weight, "seq", axis=1, tiled=True),
    )
    key_width = full_length // 8
    score_scale = HEAD_WIDTH ** (-0.5)
    query_position = seq_index * local_length + jnp.arange(local_length, dtype=jnp.int32)
    last_needed = (seq_index + 1) * local_length

    def one_sequence(operands):
        own_queries, every_key, every_value = operands
        queries = own_queries.reshape(local_length, local_heads, HEAD_WIDTH)
        pieces = []
        for number in range(8):
            block_start = number * key_width
            compute = partial(
                score_block, queries, every_key, query_position, block_start, key_width, score_scale
            )
            skipped = partial(
                jnp.full, (local_heads, local_length, key_width), masked_score, jnp.float32
            )
            pieces.append(lax.cond(block_start < last_needed, compute, skipped))
        scores = jnp.concatenate(pieces, axis=2)
        row_peak = jnp.max(scores, axis=2, keepdims=True)
        weights = jnp.exp(scores - row_peak)
        totals = jnp.sum(weights, axis=2, keepdims=True)
        rounded = weights.astype(jnp.bfloat16)
        mixed_rows = jnp.zeros((local_length, local_heads, HEAD_WIDTH), jnp.float32)
        for number in range(8):
            block_start = number * key_width
            product = partial(value_block, rounded, every_value, block_start, key_width)
            nothing = partial(jnp.zeros, (local_length, local_heads, HEAD_WIDTH), jnp.float32)
            mixed_rows = mixed_rows + lax.cond(block_start < last_needed, product, nothing)
        attended = (mixed_rows / totals.transpose(1, 0, 2)).astype(jnp.bfloat16)
        return attended.reshape(local_length, local_heads * HEAD_WIDTH)

    attended = lax.map(one_sequence, (query_rows, whole_keys, whole_values))
    flat_attended = attended.reshape(batch_count * local_length, local_heads * HEAD_WIDTH)
    projected = lax.psum_scatter(
        jnp.dot(flat_attended, whole_proj, preferred_element_type=jnp.float32).astype(jnp.bfloat16),
        "role",
        scatter_dimension=0,
        tiled=True,
    ).astype(jnp.float32)
    hidden = residual[0].astype(jnp.float32) + projected
    variance = jnp.mean(hidden * hidden, axis=-1, keepdims=True)
    normed = (hidden * lax.rsqrt(variance + epsilon) * norm_gain).astype(jnp.bfloat16)
    expert_ids = route_experts.reshape(-1)
    gate_values = route_gates.reshape(-1)
    experts_local = gate_weight.shape[0]
    device_count = seq_count * role_count
    expert_count = experts_local * device_count
    assign = expert_ids.shape[0]
    capacity = assign // expert_count + 1
    onehot = (expert_ids[:, None] == jnp.arange(expert_count, dtype=jnp.int32)[None, :]).astype(
        jnp.int32
    )
    earlier = jnp.cumsum(onehot, axis=0) - onehot
    slot_rank = jnp.sum(earlier * onehot, axis=1)
    slot_index = expert_ids * capacity + slot_rank
    source_token = jnp.arange(assign, dtype=jnp.int32) // TOPK
    slot_token = jnp.zeros((expert_count * capacity,), jnp.int32).at[slot_index].set(source_token)
    slot_used = jnp.zeros((expert_count * capacity,), jnp.bfloat16).at[slot_index].set(1.0)
    outgoing = (normed[slot_token] * slot_used[:, None]).reshape(
        device_count, experts_local, capacity, D
    )
    incoming = lax.all_to_all(outgoing, ("seq", "role"), split_axis=0, concat_axis=0, tiled=True)
    gate_hidden = jnp.einsum(
        "sjcd,jdf->sjcf", incoming, gate_weight, preferred_element_type=jnp.float32
    )
    up_hidden = jnp.einsum(
        "sjcd,jdf->sjcf", incoming, up_weight, preferred_element_type=jnp.float32
    )
    activated = (jax.nn.silu(gate_hidden) * up_hidden).astype(jnp.bfloat16)
    returned = lax.all_to_all(
        jnp.einsum(
            "sjcf,jfd->sjcd", activated, down_weight, preferred_element_type=jnp.float32
        ).astype(jnp.bfloat16),
        ("seq", "role"),
        split_axis=0,
        concat_axis=0,
        tiled=True,
    )
    gathered = returned.reshape(expert_count * capacity, D)[slot_index]
    weighted = gathered.astype(jnp.float32) * gate_values[:, None]
    expert_sum = jnp.sum(weighted.reshape(-1, TOPK, D), axis=1)
    return (hidden + expert_sum).astype(jnp.bfloat16).reshape(residual.shape)


def solution(mesh):
    placed = (
        P("groups", "seq", "role"),
        P("groups", ("seq", "role"), None),
        P("groups", ("seq", "role"), None),
        P("role", "seq"),
        P(("groups", "role"), "seq", None),
        P(),
        P(("groups", "role"), "seq", None),
        P(("groups", "role"), "seq", None),
        P(("seq", "role"), None, None),
        P(("seq", "role"), None, None),
        P(("seq", "role"), None, None),
    )
    return jax.shard_map(
        shards,
        mesh=mesh,
        in_specs=placed,
        out_specs=P(("groups", "role"), "seq", None),
        check_vma=False,
    )
```

profile of v0, /device:TPU:0, one launch (start us, length us, event | category | flops | bytes accessed | tf_op | source)
XLA Modules:
  0.0 386.6 jit_solution(5642459190348767778)
XLA Ops:
  7.4 16.0 %all_gather.15 = bf16[4,64,512]{2,1,0:T(8,128)(2,1)S(1)} all-gather(bf16[4,16,512]{2,1,0:T(8,128)(2,1)} %param.46), channel_id=1, replica_groups=mesh['groups'=2,'seq'=4,'role'=4] {'role'}, dimensions={1}, use_global_device_ids=true | all-gather | bytes 327680 | tf_op jit(solution)/shard_map/all_gather | solution.py:61
  23.4 8.1 %all_gather.16 = bf16[4,256,128]{2,1,0:T(8,128)(2,1)} all-gather(bf16[4,64,128]{2,1,0:T(8,128)(2,1)S(1)} %constant_dynamic-slice_fusion.1), channel_id=1, replica_groups=mesh['groups'=2,'seq'=4,'role'=4] {'seq'}, dimensions={1}, use_global_device_ids=true | all-gather | bytes 327680 | tf_op jit(solution)/shard_map/all_gather | solution.py:67
  31.5 14.5 %all_gather.17 = bf16[4,64,512]{2,1,0:T(8,128)(2,1)S(1)} all-gather(bf16[4,16,512]{2,1,0:T(8,128)(2,1)} %param.47), channel_id=1, replica_groups=mesh['groups'=2,'seq'=4,'role'=4] {'role'}, dimensions={1}, use_global_device_ids=true | all-gather | bytes 327680 | tf_op jit(solution)/shard_map/all_gather | solution.py:62
  46.0 6.2 %all_gather.18 = bf16[4,256,128]{2,1,0:T(8,128)(2,1)} all-gather(bf16[4,64,128]{2,1,0:T(8,128)(2,1)S(1)} %constant_dynamic-slice_fusion), channel_id=1, replica_groups=mesh['groups'=2,'seq'=4,'role'=4] {'seq'}, dimensions={1}, use_global_device_ids=true | all-gather | bytes 327680 | tf_op jit(solution)/shard_map/all_gather | solution.py:68
  52.2 92.0 %while.13 = (s32[]{:T(128)}, bf16[4,64,1024]{2,1,0:T(8,128)(2,1)}, pred[]{:T(512)}, bf16[4,256,128]{2,1,0:T(8,128)(2,1)}, bf16[4,64,1024]{2,1,0:T(8,128)(2,1)}, ...) while((s32[]{:T(128)}, bf16[4,64,1024]{2,1,0:T(8,128)(2,1)}, ...), condition=%wide.region_42.43_spmd.clone, body=%wide.region_0.42_spmd.clone.sunk | while | flops 68500768 | bytes 10589201 | solution.py:103
  56.7 1.3 fusion.131
  58.1 1.3 fusion.132
  59.3 1.3 fusion.133
  60.6 1.3 fusion.134
  63.3 2.2 fusion.136
  68.6 1.8 conditional.62
  68.6 1.8 convolution_bitcast_fusion
  70.3 1.8 conditional.63
  70.3 1.8 convolution_bitcast_fusion.1
  72.8 1.6 divide_convert_fusion.2
  79.8 1.3 fusion.131
  81.1 1.3 fusion.132
  82.4 1.3 fusion.133
  83.6 1.3 fusion.134
  86.3 2.2 fusion.136
  91.6 1.8 conditional.62
  91.6 1.8 convolution_bitcast_fusion
  93.3 1.8 conditional.63
  93.3 1.8 convolution_bitcast_fusion.1
  95.8 1.6 divide_convert_fusion.2
  102.8 1.3 fusion.131
  104.1 1.3 fusion.132
  105.4 1.3 fusion.133
  106.7 1.3 fusion.134
  109.3 2.2 fusion.136
  114.6 1.8 conditional.62
  114.6 1.8 convolution_bitcast_fusion
  116.3 1.8 conditional.63
  116.3 1.8 convolution_bitcast_fusion.1
  118.8 1.6 divide_convert_fusion.2
  125.8 1.3 fusion.131
  127.1 1.3 fusion.132
  128.4 1.3 fusion.133
  129.7 1.3 fusion.134
  132.4 2.2 fusion.136
  137.6 1.8 conditional.62
  137.6 1.8 convolution_bitcast_fusion
  139.4 1.8 conditional.63
  139.4 1.8 convolution_bitcast_fusion.1
  141.9 1.6 divide_convert_fusion.2
  144.3 4.6 %convolution_convert_fusion.1 = bf16[256,2048]{1,0:T(8,128)(2,1)} fusion(bf16[256,1024]{1,0:T(8,128)(2,1)} %bitcast.244, bf16[1024,2048]{1,0:T(8,128)(2,1)} %all-gather.2.cloned.1.call-done), kind=kOutput, calls=%fused_computation.130 | convolution fusion | flops 1074266112 | bytes 5767168 | tf_op jit(solution)/shard_map/dot_general | solution.py:106
  149.2 1.2 reduce-window.6
  150.9 2.4 scatter_custom_fusion
  153.4 3.8 scatter_custom_fusion.1
  157.3 52.8 %reduce-scatter.2.cloned.1.call-done = bf16[64,2048]{1,0:T(8,128)(2,1)} async-done(((bf16[256,2048]{1,0:T(8,128)(2,1)}), bf16[64,2048]{1,0:T(8,128)(2,1)}) %reduce-scatter.2.cloned.1.call-update) | async-done | bytes 262160 | tf_op jit(solution)/shard_map/reduce_scatter | solution.py:105
  210.1 1.1 multiply_reduce_fusion
  211.3 1.1 multiply_convert_fusion
  212.4 3.9 %gather_fusion = bf16[528,2048]{1,0:T(8,128)(2,1)} fusion(bf16[64,2048]{1,0:T(8,128)(2,1)S(1)} %multiply_convert_fusion, s32[1024]{0:T(1024)S(1)} %pad_clamp_fusion.1), kind=kCustom, calls=%fused_computation | custom fusion | bytes 4327488 | tf_op jit(solution)/shard_map/gather | solution.py:130
  216.3 3.1 gather.9
  219.4 2.0 multiply_bitcast_fusion
  221.4 63.9 %all_to_all.10 = bf16[16,1,33,2048]{3,2,1,0:T(8,128)(2,1)S(1)} all-to-all(bf16[16,1,33,2048]{3,2,1,0:T(8,128)(2,1)S(1)} %multiply_bitcast_fusion), channel_id=1, replica_groups=mesh['groups'=2,'seq'=4,'role'=4] {'seq','role'}, dimensions={0} | all-to-all | bytes 4325376 | tf_op jit(solution)/shard_map/all_to_all | solution.py:133
  285.3 1.5 copy-done.1
  286.8 3.6 fusion.72
  290.4 9.7 %fusion.74 = bf16[16,1,33,2048]{3,2,1,0:T(8,128)(2,1)} fusion(bf16[1,768,2048]{2,1,0:T(8,128)(2,1)S(1)} %copy-done, bf16[1,2048,768]{2,1,0:T(8,128)(2,1)} %param.54, bf16[16,1,33,2048]{3,2,1,0:T(8,128)(2,1)} %copy-done.1, f32[16,33,768]{2,1,0:T(8,128)} %fusion.72), kind=kOutput, calls=%fused_computation.126 | convolution fusion | flops 3325403136 | bytes 12238848 | tf_op jit(solution)/shard_map/sjcf,jfd->sjcd/dot_general | solution.py:142
  300.1 4.6 %all-to-all-start.1 = ((bf16[16,1,33,2048]{3,2,1,0:T(8,128)(2,1)}), bf16[16,1,33,2048]{3,2,1,0:T(8,128)(2,1)}, u32[]{:S(2)}, u32[]{:S(2)}) async-start(bf16[16,1,33,2048]{3,2,1,0:T(8,128)(2,1)} %fusion.74), calls=%async_computation.2 | async-start | bytes 5242880 | tf_op jit(solution)/shard_map/all_to_all | solution.py:141
  304.8 60.5 %all-to-all-done.1 = bf16[16,1,33,2048]{3,2,1,0:T(8,128)(2,1)} async-done(((bf16[16,1,33,2048]{3,2,1,0:T(8,128)(2,1)}), bf16[16,1,33,2048]{3,2,1,0:T(8,128)(2,1)}, u32[]{:S(2)}, u32[]{:S(2)}) %all-to-all-start.1) | async-done | bytes 2162720 | tf_op jit(solution)/shard_map/all_to_all | solution.py:141
  365.3 3.1 reshape.428
  368.4 7.1 %gather_fusion.1 = bf16[512,2048]{1,0:T(8,128)(2,1)} fusion(bf16[528,2048]{1,0:T(8,128)(2,1)} %reshape.428, s32[1024]{0:T(1024)S(1)} %pad_clamp_fusion), kind=kCustom, calls=%fused_computation.1 | custom fusion | bytes 4196352 | tf_op jit(solution)/shard_map/gather | solution.py:150
  375.5 3.5 fusion.68
  (218 shorter events, 61.5 us)
Async XLA Ops:
  6.5 283.9 %copy-start = (bf16[1,768,2048]{2,1,0:T(8,128)(2,1)S(1)}, bf16[1,768,2048]{2,1,0:T(8,128)(2,1)}, u32[]{:S(2)}) copy-start(bf16[1,768,2048]{2,1,0:T(8,128)(2,1)} %param.55) | copy-start | bytes 9437188
  6.5 137.7 %all-gather.2.cloned.1.call-start = ((), (), s32[]{:S(2)}) async-start(), calls=%async_computation.3 | async-start | bytes 5242880 | tf_op jit(solution)/shard_map/all_gather | solution.py:69
  7.3 202.9 %reduce-scatter.2.cloned.1.call-start = ((), (), s32[]{:S(2)}) async-start(), calls=%async_computation.4 | async-start | bytes 1310720 | tf_op jit(solution)/shard_map/reduce_scatter | solution.py:105
  144.3 4.6 %copy-start.5 = (s32[1,64,8]{1,2,0:T(8,128)S(1)}, s32[1,64,8]{1,2,0:T(8,128)}, u32[]{:S(2)}) copy-start(s32[1,64,8]{1,2,0:T(8,128)} %param.51) | copy-start | bytes 6148
  144.3 65.9 %copy-start.2 = (bf16[1,64,2048]{2,1,0:T(8,128)(2,1)S(1)}, bf16[1,64,2048]{2,1,0:T(8,128)(2,1)}, u32[]{:S(2)}) copy-start(bf16[1,64,2048]{2,1,0:T(8,128)(2,1)} %param.49) | copy-start | bytes 786436
  144.3 67.0 %copy-start.6 = (f32[2048]{0:T(1024)S(1)}, f32[2048]{0:T(1024)}, u32[]{:S(2)}) copy-start(f32[2048]{0:T(1024)} %param.50) | copy-start | bytes 24580
  221.4 65.4 %copy-start.8 = (bf16[1,2048,768]{2,1,0:T(8,128)(2,1)S(1)}, bf16[1,2048,768]{2,1,0:T(8,128)(2,1)}, u32[]{:S(2)}) copy-start(bf16[1,2048,768]{2,1,0:T(8,128)(2,1)} %param.53) | copy-start | bytes 9437188
  285.3 1.5 copy-start.1
  300.1 4.6 %copy-start.7 = (f32[1,64,8]{1,2,0:T(8,128)S(1)}, f32[1,64,8]{1,2,0:T(8,128)}, u32[]{:S(2)}) copy-start(f32[1,64,8]{1,2,0:T(8,128)} %param.52) | copy-start | bytes 6148
  300.1 65.2 %all-to-all-start.1 = ((bf16[16,1,33,2048]{3,2,1,0:T(8,128)(2,1)}), bf16[16,1,33,2048]{3,2,1,0:T(8,128)(2,1)}, u32[]{:S(2)}, u32[]{:S(2)}) async-start(bf16[16,1,33,2048]{3,2,1,0:T(8,128)(2,1)} %fusion.74), calls=%async_computation.2 | async-start | bytes 5242880 | tf_op jit(solution)/shard_map/all_to_all | solution.py:141
  375.5 3.5 copy-start.3
  375.5 3.5 copy-start.4
Sparse Core Ops, SparseCore 0:
  8.9 38.5 all-gather.1
  149.0 61.0 reduce-scatter.1
where the time goes:
time: 389 us; the launch traced here: 387 us
  waiting for transfers between devices  114 us (29%)
  blocking collectives  109 us (28%)
  other arithmetic  59.6 us (15%)
  local copies, waits for them, and re-layouts  51.3 us (13%)
  matrix products  33.9 us (9%)
  between operations  13.6 us (3%)
  starting transfers between devices  4.63 us (1%)
    all_to_all x1, blocking collectives, shards(): lax.all_to_all(outgoing, ('seq', 'role'), split_axis=0, concat_axis=0, ti...  63.9 us
    all_to_all x1, waiting for transfers between devices, shards(): lax.all_to_all(jnp.einsum('sjcf,jfd->sjcd', activated, down_weight, prefe...  60.5 us
    reduce_scatter x1, waiting for transfers between devices, shards(): lax.psum_scatter(jnp.dot(flat_attended, whole_proj, preferred_element_typ...  52.8 us
    reduce_max x36, other arithmetic, one_sequence(): row_peak = jnp.max(scores, axis=2, keepdims=True)  34.1 us
    all_gather x1, blocking collectives, shards(): lax.all_gather(encoded_key_rows, 'role', axis=1, tiled=True)  16 us
    another operation x49, local copies, waits for them, and re-layouts  14.9 us
    all_gather x1, blocking collectives, shards(): lax.all_gather(value_matrix_rows, 'role', axis=1, tiled=True)  14.5 us
    dot_general x8, matrix products, value_block(): jnp.einsum('hqk,kd->qhd', prob_block, values_part, preferred_element_type...  14.2 us
  transfers between devices with their start and end apart: 3, of which 2 were waited for; matrix products, arithmetic and copies ran while one was open for 26% of the time, Pallas kernels for 0%

commit v1 on v0

--- a/solution.py
+++ b/solution.py
@@ -3,6 +3,8 @@
 import jax
 import jax.numpy as jnp
 from jax import lax
+from jax.experimental import pallas as pl
+from jax.experimental.pallas import tpu as pltpu
 from jax.sharding import PartitionSpec as P
 
 D = 2048
@@ -153,7 +155,490 @@
     return (hidden + expert_sum).astype(jnp.bfloat16).reshape(residual.shape)
 
 
+MESH = pl.DeviceIdType.MESH
+LANES = 128
+
+
+def aligned(index, size):
+    return pl.ds(pl.multiple_of(index * size, size), size)
+
+
+def layer_kernel(
+    roles,
+    seqs,
+    q_hbm,
+    k_hbm,
+    v_hbm,
+    wo_hbm,
+    res_hbm,
+    gain_hbm,
+    ids_hbm,
+    gates_hbm,
+    gw_hbm,
+    uw_hbm,
+    dw_hbm,
+    out_ref,
+    q,
+    kv,
+    wo,
+    res,
+    gain,
+    ids,
+    gates,
+    gw,
+    uw,
+    dw,
+    att,
+    part,
+    part_in,
+    hid,
+    tok,
+    act,
+    y,
+    y_core,
+    y_x,
+    y_role,
+    load_sem,
+    own_sem,
+    kv1_s,
+    kv1_r,
+    kv2_s,
+    kv2_r,
+    wo_s,
+    wo_r,
+    pr_s,
+    pr_r,
+    tz_s,
+    tz_r,
+    tx_s,
+    tx_r,
+    tc_s,
+    tc_r,
+    yc_s,
+    yc_r,
+    yx_s,
+    yx_r,
+    yz_s,
+    yz_r,
+):
+    s = lax.axis_index("seq")
+    r = lax.axis_index("role")
+    mate = s + 1 - 2 * (s % 2)
+    side = (s + 2) % 4
+    far = mate + 2 - 4 * (mate // 2)
+    batch, rows, width = q.shape
+    heads = width // HEAD_WIDTH
+    own_keys = k_hbm.shape[1]
+    full = rows * seqs
+    cols = wo.shape[2]
+    offs = (2, 1, 3)
+
+    def remote(src, dst, ssem, rsem, device):
+        return pltpu.make_async_remote_copy(
+            src_ref=src,
+            dst_ref=dst,
+            send_sem=ssem,
+            recv_sem=rsem,
+            device_id=device,
+            device_id_type=MESH,
+        )
+
+    def to_role(off):
+        return {"role": (r + off) % roles}
+
+    barrier = pltpu.get_barrier_semaphore()
+    for off in offs:
+        pl.semaphore_signal(barrier, inc=1, device_id=to_role(off), device_id_type=MESH)
+    for peer in (mate, side):
+        pl.semaphore_signal(barrier, inc=1, device_id={"seq": peer}, device_id_type=MESH)
+
+    loads = [
+        pltpu.make_async_copy(a, b, load_sem.at[i])
+        for i, (a, b) in enumerate(
+            (
+                (q_hbm, q),
+                (res_hbm, res),
+                (gain_hbm, gain),
+                (ids_hbm, ids),
+                (gates_hbm, gates),
+                (wo_hbm, wo.at[s]),
+                (gw_hbm, gw),
+                (uw_hbm, uw),
+                (dw_hbm, dw),
+            )
+        )
+    ]
+    pair = (k_hbm, v_hbm)
+
+    def kv_spot(t, seq, role):
+        return kv.at[t, :, aligned(seq * roles + role, own_keys), :]
+
+    owns = [
+        pltpu.make_async_copy(
+            pair[t].at[:, :, aligned(r, HEAD_WIDTH)], kv_spot(t, s, r), own_sem.at[t]
+        )
+        for t in range(2)
+    ]
+    for copy in owns + loads[:6]:
+        copy.start()
+    pl.semaphore_wait(barrier, roles - 1 + 2)
+
+    def kv1(t, off):
+        return remote(
+            pair[t].at[:, :, aligned((r + off) % roles, HEAD_WIDTH)],
+            kv_spot(t, s, r),
+            kv1_s.at[t, off],
+            kv1_r.at[t, off],
+            to_role(off),
+        )
+
+    def kv1_in(t, off):
+        source = (r + roles - off) % roles
+        return remote(
+            pair[t].at[:, :, aligned(r, HEAD_WIDTH)],
+            kv_spot(t, s, source),
+            kv1_s.at[t, off],
+            kv1_r.at[t, off],
+            to_role(off),
+        )
+
+    for off in offs:
+        for t in range(2):
+            kv1(t, off).start()
+    for copy in loads[6:]:
+        copy.start()
+
+    def kv2(t, path, seq, target):
+        spot = kv.at[t, :, aligned(seq, rows), :]
+        return remote(spot, spot, kv2_s.at[t, path], kv2_r.at[t, path], {"seq": target})
+
+    def wo2(path, seq, target):
+        return remote(wo.at[seq], wo.at[seq], wo_s.at[path], wo_r.at[path], {"seq": target})
+
+    for copy in owns:
+        copy.wait()
+    for off in offs:
+        for t in range(2):
+            kv1_in(t, off).wait_recv()
+    for t in range(2):
+        kv2(t, 1, s, side).start()
+        kv2(t, 0, s, mate).start()
+    loads[5].wait()
+    wo2(1, s, side).start()
+    wo2(0, s, mate).start()
+
+    for copy in loads[:5]:
+        copy.wait()
+    lane = lax.broadcasted_iota(jnp.int32, (rows, LANES), 1)
+    table = jnp.zeros((rows, LANES), jnp.float32)
+    for k in range(ids.shape[2]):
+        chosen = lane % (LANES // 2) == ids[0, :, k : k + 1]
+        table = table + jnp.where(chosen, gates[0, :, k : k + 1], 0.0)
+    high = table.astype(jnp.bfloat16)
+    low = (table - high.astype(jnp.float32)).astype(jnp.bfloat16)
+    depth = hid.shape[1]
+    tok[r, aligned(s, rows), depth : depth + LANES] = jnp.where(
+        lane < LANES // 2, high.astype(jnp.float32), low.astype(jnp.float32)
+    ).astype(jnp.bfloat16)
+
+    for t in range(2):
+        kv2(t, 1, side, side).wait_recv()
+        kv2(t, 2, side, mate).start()
+    for t in range(2):
+        kv2(t, 0, mate, mate).wait_recv()
+        kv2(t, 2, far, mate).wait_recv()
+
+    query_row = s * rows + lax.broadcasted_iota(jnp.int32, (rows, full), 0)
+    allowed = lax.broadcasted_iota(jnp.int32, (rows, full), 1) <= query_row
+
+    def attend(b, carry):
+        keys, values = kv[0, b], kv[1, b]
+        for h in range(heads):
+            head = pl.ds(h * HEAD_WIDTH, HEAD_WIDTH)
+            scores = lax.dot_general(
+                q[b, :, head],
+                keys,
+                (((1,), (1,)), ((), ())),
+                preferred_element_type=jnp.float32,
+            ) * (HEAD_WIDTH**-0.5)
+            scores = jnp.where(allowed, scores, masked_score)
+            weights = jnp.exp(scores - jnp.max(scores, axis=1, keepdims=True))
+            totals = jnp.sum(weights, axis=1, keepdims=True)
+            mixed = jnp.dot(
+                weights.astype(jnp.bfloat16), values, preferred_element_type=jnp.float32
+            )
+            att[aligned(b, rows), head] = (mixed / totals).astype(jnp.bfloat16)
+        return carry
+
+    lax.fori_loop(0, batch, attend, 0)
+
+    def pr(j, off):
+        return remote(
+            part.at[j, aligned((r + off) % roles, rows), :],
+            part_in.at[j, off],
+            pr_s.at[j, off],
+            pr_r.at[j, off],
+            to_role(off),
+        )
+
+    def project(j):
+        part[j] = jnp.dot(att[...], wo[j], preferred_element_type=jnp.float32).astype(
+            jnp.bfloat16
+        )
+        for off in offs:
+            pr(j, off).start()
+
+    project(s)
+    wo2(0, mate, mate).wait_recv()
+    project(mate)
+    wo2(1, side, side).wait_recv()
+    wo2(2, side, mate).start()
+    project(side)
+    wo2(2, far, mate).wait_recv()
+    project(far)
+
+    square = jnp.zeros((rows, 1), jnp.float32)
+    for j in range(seqs):
+        block = pl.ds(j * cols, cols)
+        total = part[j, aligned(r, rows), :].astype(jnp.float32)
+        for off in offs:
+            pr(j, off).wait_recv()
+            total = total + part_in[j, off].astype(jnp.float32)
+        hidden = res[0, :, block].astype(jnp.float32) + total
+        hid[:, block] = hidden
+        square = square + jnp.sum(hidden * hidden, axis=1, keepdims=True)
+    scale = lax.rsqrt(square / depth + epsilon)
+    for j in range(seqs):
+        block = pl.ds(j * cols, cols)
+        tok[r, aligned(s, rows), block] = (hid[:, block] * scale * gain[:, block]).astype(
+            jnp.bfloat16
+        )
+
+    def piece(seq, role):
+        return tok.at[role, aligned(seq, rows), :]
+
+    def tz(off):
+        return remote(piece(s, r), piece(s, r), tz_s.at[off], tz_r.at[off], to_role(off))
+
+    def tz_in(off, role):
+        return remote(piece(s, role), piece(s, role), tz_s.at[off], tz_r.at[off], to_role(off))
+
+    def tx(i, seq, role):
+        return remote(
+            piece(seq, role), piece(seq, role), tx_s.at[i], tx_r.at[i], {"seq": side}
+        )
+
+    def tc(i, path, seq, role):
+        return remote(
+            piece(seq, role), piece(seq, role), tc_s.at[i, path], tc_r.at[i, path], {"seq": mate}
+        )
+
+    def yc(i, path, role):
+        seq = far if path else mate
+        return remote(
+            y.at[role, aligned(seq, rows), :],
+            y_core.at[i, path],
+            yc_s.at[i, path],
+            yc_r.at[i, path],
+            {"seq": mate},
+        )
+
+    def yx(i, role):
+        return remote(
+            y.at[role, aligned(side, rows), :], y_x.at[i], yx_s.at[i], yx_r.at[i], {"seq": side}
+        )
+
+    def yz(off, role):
+        return remote(
+            y.at[role, aligned(s, rows), :],
+            y_role.at[off],
+            yz_s.at[off],
+            yz_r.at[off],
+            {"role": role},
+        )
+
+    tx(0, s, r).start()
+    for off in offs:
+        tz(off).start()
+    tc(0, 0, s, r).start()
+    for copy in loads[6:]:
+        copy.wait()
+
+    expert = s * roles + r
+    hidden_width = act.shape[1]
+    step_f = hidden_width // 3 if hidden_width % 3 == 0 else hidden_width
+    gate_lane = lax.broadcasted_iota(jnp.int32, (full, LANES), 1) % (LANES // 2)
+
+    def off_of(i):
+        return (2 * i) % 3 + 3 * (i // 3)
+
+    def role_of(i):
+        return (r + roles - off_of(i)) % roles
+
+    def pass_core(i):
+        role = role_of(i)
+        yc(i, 0, role).wait_recv()
+        yc(i, 1, role).wait_recv()
+        spot = aligned(side, rows)
+        y[role, spot, :] = (
+            y[role, spot, :].astype(jnp.float32) + y_core[i, 1].astype(jnp.float32)
+        ).astype(jnp.bfloat16)
+        yx(i, role).start()
+
+    def summed(i):
+        role = role_of(i)
+        yx(i, role).wait_recv()
+        return (
+            y[role, aligned(s, rows), :].astype(jnp.float32)
+            + y_core[i, 0].astype(jnp.float32)
+            + y_x[i].astype(jnp.float32)
+        )
+
+    def pass_role(i):
+        role = role_of(i)
+        y[role, aligned(s, rows), :] = summed(i).astype(jnp.bfloat16)
+        yz(off_of(i), role).start()
+
+    def one_block(i, carry):
+        role = role_of(i)
+
+        @pl.when(i > 0)
+        def _():
+            tz_in(off_of(i), role).wait_recv()
+            tx(i, s, role).start()
+            tc(i, 0, s, role).start()
+
+        tx(i, side, role).wait_recv()
+        tc(i, 1, side, role).start()
+        tc(i, 0, mate, role).wait_recv()
+        tc(i, 1, far, role).wait_recv()
+
+        shares = tok[role, :, depth : depth + LANES].astype(jnp.float32)
+        share = jnp.sum(jnp.where(gate_lane == expert, shares, 0.0), axis=1, keepdims=True)
+        inputs = tok[role, :, 0:depth]
+        for start in range(0, hidden_width, step_f):
+            block = pl.ds(start, step_f)
+            gate = jnp.dot(inputs, gw[0, :, block], preferred_element_type=jnp.float32)
+            up = jnp.dot(inputs, uw[0, :, block], preferred_element_type=jnp.float32)
+            act[:, block] = (gate / (1.0 + jnp.exp(-gate)) * up).astype(jnp.bfloat16)
+        for j in range(seqs):
+            block = pl.ds(j * cols, cols)
+            product = jnp.dot(act[...], dw[0, :, block], preferred_element_type=jnp.float32)
+            y[role, :, block] = (product * share).astype(jnp.bfloat16)
+        yc(i, 1, role).start()
+        yc(i, 0, role).start()
+
+        @pl.when(i > 0)
+        def _():
+            pass_core(i - 1)
+
+        @pl.when(i > 2)
+        def _():
+            pass_role(i - 2)
+
+        return carry
+
+    lax.fori_loop(0, roles, one_block, 0)
+    pass_core(roles - 1)
+    pass_role(roles - 2)
+    pass_role(roles - 1)
+    total = hid[...] + summed(0)
+    for off in offs:
+        yz(off, r).wait_recv()
+        total = total + y_role[off].astype(jnp.float32)
+    out_ref[0] = total.astype(out_ref.dtype)
+
+    for off in offs:
+        for t in range(2):
+            kv1(t, off).wait_send()
+        for j in range(seqs):
+            pr(j, off).wait_send()
+        tz(off).wait_send()
+        yz(off, r).wait_send()
+    for path in range(3):
+        for t in range(2):
+            kv2(t, path, s, mate).wait_send()
+        wo2(path, s, mate).wait_send()
+    for i in range(roles):
+        tx(i, s, r).wait_send()
+        yx(i, r).wait_send()
+        for path in range(2):
+            tc(i, path, s, r).wait_send()
+            yc(i, path, r).wait_send()
+
+
+def fused(
+    query_rows,
+    encoded_key_rows,
+    value_matrix_rows,
+    output_weight,
+    residual,
+    norm_gain,
+    route_experts,
+    route_gates,
+    gate_weight,
+    up_weight,
+    down_weight,
+):
+    seqs, roles = lax.axis_size("seq"), lax.axis_size("role")
+    batch, rows, width = query_rows.shape
+    depth, cols = residual.shape[2], output_weight.shape[1]
+    hidden_width = gate_weight.shape[2]
+    full = rows * seqs
+    bf16, f32 = jnp.bfloat16, jnp.float32
+    gain = norm_gain.reshape(1, depth)
+    vmem = [
+        pltpu.VMEM(query_rows.shape, bf16),
+        pltpu.VMEM((2, batch, full, HEAD_WIDTH), bf16),
+        pltpu.VMEM((seqs, width, cols), bf16),
+        pltpu.VMEM(residual.shape, bf16),
+        pltpu.VMEM(gain.shape, f32),
+        pltpu.VMEM(route_experts.shape, jnp.int32),
+        pltpu.VMEM(route_gates.shape, f32),
+        pltpu.VMEM(gate_weight.shape, bf16),
+        pltpu.VMEM(up_weight.shape, bf16),
+        pltpu.VMEM(down_weight.shape, bf16),
+        pltpu.VMEM((batch * rows, width), bf16),
+        pltpu.VMEM((seqs, batch * rows, cols), bf16),
+        pltpu.VMEM((seqs, roles, rows, cols), bf16),
+        pltpu.VMEM((rows, depth), f32),
+        pltpu.VMEM((roles, full, depth + LANES), bf16),
+        pltpu.VMEM((full, hidden_width), bf16),
+        pltpu.VMEM((roles, full, depth), bf16),
+        pltpu.VMEM((roles, 2, rows, depth), bf16),
+        pltpu.VMEM((roles, rows, depth), bf16),
+        pltpu.VMEM((roles, rows, depth), bf16),
+    ]
+    dma = pltpu.SemaphoreType.DMA
+    counts = [(2, roles)] * 2 + [(2, 3)] * 2 + [(3,)] * 2 + [(seqs, roles)] * 2
+    counts += [(roles,)] * 4 + [(roles, 2)] * 4 + [(roles,)] * 4
+    return pl.pallas_call(
+        partial(layer_kernel, roles, seqs),
+        out_shape=jax.ShapeDtypeStruct(residual.shape, bf16),
+        in_specs=[pl.BlockSpec(memory_space=pl.ANY)] * 11,
+        out_specs=pl.BlockSpec(memory_space=pltpu.VMEM),
+        scratch_shapes=vmem + [dma((9,)), dma((2,))] + [dma(count) for count in counts],
+        compiler_params=pltpu.CompilerParams(
+            collective_id=0, has_side_effects=True, vmem_limit_bytes=60 * 1024 * 1024
+        ),
+    )(
+        query_rows,
+        encoded_key_rows,
+        value_matrix_rows,
+        output_weight,
+        residual,
+        gain,
+        route_experts,
+        route_gates,
+        gate_weight,
+        up_weight,
+        down_weight,
+    )
+
+
 def solution(mesh):
+    square = mesh.shape["seq"] == 4 and mesh.shape["role"] == KEY_VALUE_HEADS
+    body = fused if square else shards
     placed = (
         P("groups", "seq", "role"),
         P("groups", ("seq", "role"), None),
@@ -168,7 +653,7 @@
         P(("seq", "role"), None, None),
     )
     return jax.shard_map(
-        shards,
+        body,
         mesh=mesh,
         in_specs=placed,
         out_specs=P(("groups", "role"), "seq", None),

time: 389 us -> 141 us (0.36)
  Pallas kernels: 0 us -> 136 us
  waiting for transfers between devices: 114 us -> 0 us
  blocking collectives: 109 us -> 0 us
  other arithmetic: 59.6 us -> 0 us
  local copies, waits for them, and re-layouts: 51.3 us -> 4.42 us
  matrix products: 33.9 us -> 0 us
  between operations: 13.6 us -> 0.01 us
  starting transfers between devices: 4.63 us -> 0 us
    pallas_call x0 -> x1, Pallas kernels: none -> 136 us  [fused(): pl.pallas_call(partial(layer_kernel, roles, seqs), out_shape=jax.ShapeDty...]
    all_to_all x1 -> x0, blocking collectives: 63.9 us -> none  [shards(): lax.all_to_all(outgoing, ('seq', 'role'), split_axis=0, concat_axis=0, ti...]
    all_to_all x1 -> x0, waiting for transfers between devices: 60.5 us -> none  [shards(): lax.all_to_all(jnp.einsum('sjcf,jfd->sjcd', activated, down_weight, prefe...]
    reduce_scatter x1 -> x0, waiting for transfers between devices: 52.8 us -> none  [shards(): lax.psum_scatter(jnp.dot(flat_attended, whole_proj, preferred_element_typ...]
    all_gather x4 -> x0, blocking collectives: 44.8 us -> none  [the longest x1 16 us: shards(): lax.all_gather(encoded_key_rows, 'role', axis=1, tiled=True)]
    reduce_max x36 -> x0, other arithmetic: 34.1 us -> none  [one_sequence(): row_peak = jnp.max(scores, axis=2, keepdims=True)]
    dot_general x19 -> x0, matrix products: 33.9 us -> none  [the longest x8 14.2 us: value_block(): jnp.einsum('hqk,kd->qhd', prob_block, values_part, preferred_element_type...]
    another operation x49 -> x0, local copies, waits for them, and re-layouts: 14.9 us -> none
  transfers between devices with their start and end apart: 3 -> 0, of which waited for: 2 -> 0; matrix products, arithmetic and copies ran while one was open for 26% -> 0% of each run, Pallas kernels for 0% -> 0%
where the time goes in v1:
time: 141 us
  Pallas kernels  136 us (96%)
  local copies, waits for them, and re-layouts  4.42 us (3%)
    pallas_call x1, Pallas kernels, fused(): pl.pallas_call(partial(layer_kernel, roles, seqs), out_shape=jax.ShapeDty...  136 us
    unnamed x3, local copies, waits for them, and re-layouts  4.42 us

profile of v1, /device:TPU:0, one launch (start us, length us, event | category | flops | bytes accessed | tf_op | source)
XLA Modules:
  0.0 140.7 jit_solution(12392187164974626410)
XLA Ops:
  0.0 1.4 copy.12.ids_hbm
  1.4 1.4 copy.13.gates_hbm
  2.8 136.3 %shard_map.109 = bf16[1,64,2048]{2,1,0:T(8,128)(2,1)} custom-call(bf16[4,64,1024]{2,1,0:T(8,128)(2,1)} %q_hbm.1, bf16[4,16,512]{2,1,0:T(8,128)(2,1)} %k_hbm.1, bf16[4,16,512]{2,1,0:T(8,128)(2,1)} %v_hbm.1, bf16[1024,512]{1,0:T(8,128)(2,1)} %wo_hbm.1, bf16[1,64,2048]{2,1,0:T(8,128)(2,1)} %res_hbm.1, f32[1,2048]{1,0:T(1,128)} %bitcast.1, ...), custom_call_target="tpu_custom_call" | custom-call | tf_op jit(solution)/shard_map/pallas_call | solution.py:615
  139.1 1.7 %copy.15 = bf16[1,64,2048]{2,1,0:T(8,128)(2,1)} copy(bf16[1,64,2048]{2,1,0:T(8,128)(2,1)} %shard_map.109) | data formatting | bytes 524288

commit v2 on v1

--- a/solution.py
+++ b/solution.py
@@ -204,8 +204,12 @@
     kv1_r,
     kv2_s,
     kv2_r,
-    wo_s,
-    wo_r,
+    wm_s,
+    wm_r,
+    wx_s,
+    wx_r,
+    wy_s,
+    wy_r,
     pr_s,
     pr_r,
     tz_s,
@@ -223,6 +227,7 @@
 ):
     s = lax.axis_index("seq")
     r = lax.axis_index("role")
+    g = lax.axis_index("groups")
     mate = s + 1 - 2 * (s % 2)
     side = (s + 2) % 4
     far = mate + 2 - 4 * (mate // 2)
@@ -231,7 +236,12 @@
     own_keys = k_hbm.shape[1]
     full = rows * seqs
     cols = wo.shape[2]
-    offs = (2, 1, 3)
+    offs = (1, 2, 3)
+    chunks = 4
+    chunk_rows = width // (2 * chunks)
+
+    def role_of(i):
+        return (r // 2 + i // 2) % 2 * 2 + (r + i) % 2
 
     def remote(src, dst, ssem, rsem, device):
         return pltpu.make_async_remote_copy(
@@ -244,13 +254,13 @@
         )
 
     def to_role(off):
-        return {"role": (r + off) % roles}
+        return {"role": role_of(off)}
 
     barrier = pltpu.get_barrier_semaphore()
     for off in offs:
         pl.semaphore_signal(barrier, inc=1, device_id=to_role(off), device_id_type=MESH)
-    for peer in (mate, side):
-        pl.semaphore_signal(barrier, inc=1, device_id={"seq": peer}, device_id_type=MESH)
+    for peer in ({"seq": mate}, {"seq": side}, {"groups": 1 - g}):
+        pl.semaphore_signal(barrier, inc=1, device_id=peer, device_id_type=MESH)
 
     loads = [
         pltpu.make_async_copy(a, b, load_sem.at[i])
@@ -281,11 +291,11 @@
     ]
     for copy in owns + loads[:6]:
         copy.start()
-    pl.semaphore_wait(barrier, roles - 1 + 2)
+    pl.semaphore_wait(barrier, roles - 1 + 3)
 
     def kv1(t, off):
         return remote(
-            pair[t].at[:, :, aligned((r + off) % roles, HEAD_WIDTH)],
+            pair[t].at[:, :, aligned(role_of(off), HEAD_WIDTH)],
             kv_spot(t, s, r),
             kv1_s.at[t, off],
             kv1_r.at[t, off],
@@ -293,7 +303,7 @@
         )
 
     def kv1_in(t, off):
-        source = (r + roles - off) % roles
+        source = role_of(off)
         return remote(
             pair[t].at[:, :, aligned(r, HEAD_WIDTH)],
             kv_spot(t, s, source),
@@ -312,9 +322,33 @@
         spot = kv.at[t, :, aligned(seq, rows), :]
         return remote(spot, spot, kv2_s.at[t, path], kv2_r.at[t, path], {"seq": target})
 
-    def wo2(path, seq, target):
-        return remote(wo.at[seq], wo.at[seq], wo_s.at[path], wo_r.at[path], {"seq": target})
-
+    def wo_part(seq, n):
+        return wo.at[seq, aligned(n, chunk_rows), :]
+
+    def wo_own(seq):
+        return remote(wo.at[seq], wo.at[seq], wm_s.at[0], wm_r.at[0], {"seq": mate})
+
+    def wo_x(seq, c):
+        spot = wo_part(seq, g * chunks + c)
+        return remote(spot, spot, wx_s.at[c], wx_r.at[c], {"seq": side})
+
+    def wo_y(half, c):
+        spot = wo_part(side, half * chunks + c)
+        return remote(spot, spot, wy_s.at[c], wy_r.at[c], {"groups": 1 - g})
+
+    def wo_mate(seq, half, c, path):
+        spot = wo_part(seq, half * chunks + c)
+        sem = 1 + path * chunks + c
+        return remote(spot, spot, wm_s.at[sem], wm_r.at[sem], {"seq": mate})
+
+    def wo_pass(c):
+        wo_x(side, c).wait_recv()
+        wo_y(g, c).start()
+        wo_mate(side, g, c, 0).start()
+
+    loads[5].wait()
+    wo_x(s, 0).start()
+    wo_own(s).start()
     for copy in owns:
         copy.wait()
     for off in offs:
@@ -323,9 +357,8 @@
     for t in range(2):
         kv2(t, 1, s, side).start()
         kv2(t, 0, s, mate).start()
-    loads[5].wait()
-    wo2(1, s, side).start()
-    wo2(0, s, mate).start()
+    for c in range(1, chunks):
+        wo_x(s, c).start()
 
     for copy in loads[:5]:
         copy.wait()
@@ -348,6 +381,7 @@
         kv2(t, 0, mate, mate).wait_recv()
         kv2(t, 2, far, mate).wait_recv()
 
+    wo_pass(0)
     query_row = s * rows + lax.broadcasted_iota(jnp.int32, (rows, full), 0)
     allowed = lax.broadcasted_iota(jnp.int32, (rows, full), 1) <= query_row
 
@@ -368,42 +402,64 @@
                 weights.astype(jnp.bfloat16), values, preferred_element_type=jnp.float32
             )
             att[aligned(b, rows), head] = (mixed / totals).astype(jnp.bfloat16)
+
+        @pl.when(b == batch // 2)
+        def _():
+            wo_pass(1)
+
         return carry
 
     lax.fori_loop(0, batch, attend, 0)
 
-    def pr(j, off):
-        return remote(
-            part.at[j, aligned((r + off) % roles, rows), :],
-            part_in.at[j, off],
-            pr_s.at[j, off],
-            pr_r.at[j, off],
-            to_role(off),
+    def pr(j, kind):
+        return remote(
+            part.at[j, aligned(role_of((1, 3, 2)[kind]), rows), :],
+            part_in.at[j, kind],
+            pr_s.at[j, kind],
+            pr_r.at[j, kind],
+            to_role((1, 1, 2)[kind]),
         )
 
     def project(j):
         part[j] = jnp.dot(att[...], wo[j], preferred_element_type=jnp.float32).astype(
             jnp.bfloat16
         )
-        for off in offs:
-            pr(j, off).start()
+        pr(j, 1).start()
+        pr(j, 0).start()
+
+    def pass_pair(j):
+        pr(j, 1).wait_recv()
+        spot = aligned(role_of(2), rows)
+        part[j, spot, :] = (
+            part[j, spot, :].astype(jnp.float32) + part_in[j, 1].astype(jnp.float32)
+        ).astype(jnp.bfloat16)
+        pr(j, 2).start()
 
     project(s)
-    wo2(0, mate, mate).wait_recv()
+    wo_pass(2)
+    wo_own(mate).wait_recv()
     project(mate)
-    wo2(1, side, side).wait_recv()
-    wo2(2, side, mate).start()
+    wo_pass(3)
+    pass_pair(s)
+    pass_pair(mate)
+    for c in range(chunks):
+        wo_y(1 - g, c).wait_recv()
+        wo_mate(side, 1 - g, c, 1).start()
     project(side)
-    wo2(2, far, mate).wait_recv()
+    for c in range(chunks):
+        wo_mate(far, g, c, 0).wait_recv()
+        wo_mate(far, 1 - g, c, 1).wait_recv()
     project(far)
+    pass_pair(side)
+    pass_pair(far)
 
     square = jnp.zeros((rows, 1), jnp.float32)
     for j in range(seqs):
         block = pl.ds(j * cols, cols)
         total = part[j, aligned(r, rows), :].astype(jnp.float32)
-        for off in offs:
-            pr(j, off).wait_recv()
-            total = total + part_in[j, off].astype(jnp.float32)
+        for kind in (0, 2):
+            pr(j, kind).wait_recv()
+            total = total + part_in[j, kind].astype(jnp.float32)
         hidden = res[0, :, block].astype(jnp.float32) + total
         hid[:, block] = hidden
         square = square + jnp.sum(hidden * hidden, axis=1, keepdims=True)
@@ -417,11 +473,10 @@
     def piece(seq, role):
         return tok.at[role, aligned(seq, rows), :]
 
-    def tz(off):
-        return remote(piece(s, r), piece(s, r), tz_s.at[off], tz_r.at[off], to_role(off))
-
-    def tz_in(off, role):
-        return remote(piece(s, role), piece(s, role), tz_s.at[off], tz_r.at[off], to_role(off))
+    def tz(kind, role, to):
+        return remote(
+            piece(s, role), piece(s, role), tz_s.at[kind], tz_r.at[kind], {"role": to}
+        )
 
     def tx(i, seq, role):
         return remote(
@@ -448,18 +503,18 @@
             y.at[role, aligned(side, rows), :], y_x.at[i], yx_s.at[i], yx_r.at[i], {"seq": side}
         )
 
-    def yz(off, role):
-        return remote(
-            y.at[role, aligned(s, rows), :],
-            y_role.at[off],
-            yz_s.at[off],
-            yz_r.at[off],
-            {"role": role},
+    def yz(kind):
+        return remote(
+            y.at[role_of((1, 3, 2)[kind]), aligned(s, rows), :],
+            y_role.at[kind],
+            yz_s.at[kind],
+            yz_r.at[kind],
+            to_role((1, 1, 2)[kind]),
         )
 
     tx(0, s, r).start()
-    for off in offs:
-        tz(off).start()
+    tz(0, r, role_of(1)).start()
+    tz(1, r, role_of(2)).start()
     tc(0, 0, s, r).start()
     for copy in loads[6:]:
         copy.wait()
@@ -468,12 +523,6 @@
     hidden_width = act.shape[1]
     step_f = hidden_width // 3 if hidden_width % 3 == 0 else hidden_width
     gate_lane = lax.broadcasted_iota(jnp.int32, (full, LANES), 1) % (LANES // 2)
-
-    def off_of(i):
-        return (2 * i) % 3 + 3 * (i // 3)
-
-    def role_of(i):
-        return (r + roles - off_of(i)) % roles
 
     def pass_core(i):
         role = role_of(i)
@@ -494,19 +543,23 @@
             + y_x[i].astype(jnp.float32)
         )
 
-    def pass_role(i):
-        role = role_of(i)
-        y[role, aligned(s, rows), :] = summed(i).astype(jnp.bfloat16)
-        yz(off_of(i), role).start()
+    def settle(i, kind):
+        y[role_of(i), aligned(s, rows), :] = summed(i).astype(jnp.bfloat16)
+        yz(kind).start()
 
     def one_block(i, carry):
         role = role_of(i)
 
-        @pl.when(i > 0)
+        @pl.when(i < roles - 1)
         def _():
-            tz_in(off_of(i), role).wait_recv()
-            tx(i, s, role).start()
-            tc(i, 0, s, role).start()
+            following = role_of(i + 1)
+            tz(i, following, following).wait_recv()
+            tx(i + 1, s, following).start()
+            tc(i + 1, 0, s, following).start()
+
+        @pl.when(i == 1)
+        def _():
+            tz(2, role_of(2), role_of(1)).start()
 
         tx(i, side, role).wait_recv()
         tc(i, 1, side, role).start()
@@ -528,37 +581,45 @@
         yc(i, 1, role).start()
         yc(i, 0, role).start()
 
-        @pl.when(i > 0)
+        @pl.when(i > 1)
         def _():
             pass_core(i - 1)
 
-        @pl.when(i > 2)
-        def _():
-            pass_role(i - 2)
-
         return carry
 
     lax.fori_loop(0, roles, one_block, 0)
-    pass_core(roles - 1)
-    pass_role(roles - 2)
-    pass_role(roles - 1)
+    pass_core(3)
+    pass_core(0)
+    settle(1, 0)
+    second = summed(2)
+    settle(3, 1)
+    yz(1).wait_recv()
+    y[role_of(2), aligned(s, rows), :] = (second + y_role[1].astype(jnp.float32)).astype(
+        jnp.bfloat16
+    )
+    yz(2).start()
     total = hid[...] + summed(0)
-    for off in offs:
-        yz(off, r).wait_recv()
-        total = total + y_role[off].astype(jnp.float32)
+    for kind in (0, 2):
+        yz(kind).wait_recv()
+        total = total + y_role[kind].astype(jnp.float32)
     out_ref[0] = total.astype(out_ref.dtype)
 
     for off in offs:
         for t in range(2):
             kv1(t, off).wait_send()
+    for kind in range(3):
         for j in range(seqs):
-            pr(j, off).wait_send()
-        tz(off).wait_send()
-        yz(off, r).wait_send()
-    for path in range(3):
+            pr(j, kind).wait_send()
+        tz(kind, r, role_of(1)).wait_send()
+        yz(kind).wait_send()
         for t in range(2):
-            kv2(t, path, s, mate).wait_send()
-        wo2(path, s, mate).wait_send()
+            kv2(t, kind, s, mate).wait_send()
+    wo_own(s).wait_send()
+    for c in range(chunks):
+        wo_x(s, c).wait_send()
+        wo_y(g, c).wait_send()
+        for path in range(2):
+            wo_mate(s, g, c, path).wait_send()
     for i in range(roles):
         tx(i, s, r).wait_send()
         yx(i, r).wait_send()
@@ -600,18 +661,18 @@
         pltpu.VMEM(down_weight.shape, bf16),
         pltpu.VMEM((batch * rows, width), bf16),
         pltpu.VMEM((seqs, batch * rows, cols), bf16),
-        pltpu.VMEM((seqs, roles, rows, cols), bf16),
+        pltpu.VMEM((seqs, 3, rows, cols), bf16),
         pltpu.VMEM((rows, depth), f32),
         pltpu.VMEM((roles, full, depth + LANES), bf16),
         pltpu.VMEM((full, hidden_width), bf16),
         pltpu.VMEM((roles, full, depth), bf16),
         pltpu.VMEM((roles, 2, rows, depth), bf16),
         pltpu.VMEM((roles, rows, depth), bf16),
-        pltpu.VMEM((roles, rows, depth), bf16),
+        pltpu.VMEM((3, rows, depth), bf16),
     ]
     dma = pltpu.SemaphoreType.DMA
-    counts = [(2, roles)] * 2 + [(2, 3)] * 2 + [(3,)] * 2 + [(seqs, roles)] * 2
-    counts += [(roles,)] * 4 + [(roles, 2)] * 4 + [(roles,)] * 4
+    counts = [(2, roles)] * 2 + [(2, 3)] * 2 + [(9,)] * 2 + [(4,)] * 4 + [(seqs, 3)] * 2
+    counts += [(3,)] * 2 + [(roles,)] * 2 + [(roles, 2)] * 4 + [(roles,)] * 2 + [(3,)] * 2
     return pl.pallas_call(
         partial(layer_kernel, roles, seqs),
         out_shape=jax.ShapeDtypeStruct(residual.shape, bf16),
@@ -637,7 +698,7 @@
 
 
 def solution(mesh):
-    square = mesh.shape["seq"] == 4 and mesh.shape["role"] == KEY_VALUE_HEADS
+    square = mesh.shape["seq"] == 4 and mesh.shape["role"] == 4 and mesh.shape["groups"] == 2
     body = fused if square else shards
     placed = (
         P("groups", "seq", "role"),

time: 141 us -> 120 us (0.85)
  Pallas kernels: 136 us -> 115 us
    pallas_call x1, Pallas kernels: 136 us -> 115 us  [fused(): pl.pallas_call(partial(layer_kernel, roles, seqs), out_shape=jax.ShapeDty...]
where the time goes in v2:
time: 120 us
  Pallas kernels  115 us (96%)
  local copies, waits for them, and re-layouts  4.42 us (4%)
    pallas_call x1, Pallas kernels, fused(): pl.pallas_call(partial(layer_kernel, roles, seqs), out_shape=jax.ShapeDty...  115 us
    unnamed x3, local copies, waits for them, and re-layouts  4.42 us

profile of v2, /device:TPU:0, one launch (start us, length us, event | category | flops | bytes accessed | tf_op | source)
XLA Modules:
  0.0 119.9 jit_solution(893295154465135764)
XLA Ops:
  0.0 1.4 %copy.12.ids_hbm = s32[1,64,8]{2,1,0:T(8,128)} copy(s32[1,64,8]{1,2,0:T(8,128)} %param.17) | data formatting | bytes 4096 | tf_op args[6]
  1.4 1.4 %copy.13.gates_hbm = f32[1,64,8]{2,1,0:T(8,128)} copy(f32[1,64,8]{1,2,0:T(8,128)} %param.18) | data formatting | bytes 4096 | tf_op args[7]
  2.8 115.5 %shard_map.109 = bf16[1,64,2048]{2,1,0:T(8,128)(2,1)} custom-call(bf16[4,64,1024]{2,1,0:T(8,128)(2,1)} %q_hbm.1, bf16[4,16,512]{2,1,0:T(8,128)(2,1)} %k_hbm.1, bf16[4,16,512]{2,1,0:T(8,128)(2,1)} %v_hbm.1, bf16[1024,512]{1,0:T(8,128)(2,1)} %wo_hbm.1, bf16[1,64,2048]{2,1,0:T(8,128)(2,1)} %res_hbm.1, f32[1,2048]{1,0:T(1,128)} %bitcast.1, ...), custom_call_target="tpu_custom_call" | custom-call | tf_op jit(solution)/shard_map/pallas_call | solution.py:676
  118.2 1.7 %copy.15 = bf16[1,64,2048]{2,1,0:T(8,128)(2,1)} copy(bf16[1,64,2048]{2,1,0:T(8,128)(2,1)} %shard_map.109) | data formatting | bytes 524288

commit v3 on v2

--- a/solution.py
+++ b/solution.py
@@ -348,6 +348,7 @@
 
     loads[5].wait()
     wo_x(s, 0).start()
+    wo_x(s, 1).start()
     wo_own(s).start()
     for copy in owns:
         copy.wait()
@@ -357,21 +358,28 @@
     for t in range(2):
         kv2(t, 1, s, side).start()
         kv2(t, 0, s, mate).start()
-    for c in range(1, chunks):
+    for c in range(2, chunks):
         wo_x(s, c).start()
 
     for copy in loads[:5]:
         copy.wait()
-    lane = lax.broadcasted_iota(jnp.int32, (rows, LANES), 1)
-    table = jnp.zeros((rows, LANES), jnp.float32)
-    for k in range(ids.shape[2]):
-        chosen = lane % (LANES // 2) == ids[0, :, k : k + 1]
-        table = table + jnp.where(chosen, gates[0, :, k : k + 1], 0.0)
-    high = table.astype(jnp.bfloat16)
-    low = (table - high.astype(jnp.float32)).astype(jnp.bfloat16)
+    place = lax.broadcasted_iota(jnp.int32, (LANES, rows), 0)
+    table = jnp.zeros((LANES, rows), jnp.float32)
+    for k in range(ids.shape[1]):
+        chosen = place % (LANES // 2) == ids[0, k : k + 1, :]
+        table = table + jnp.where(chosen, gates[0, k : k + 1, :], 0.0)
+    high = table.astype(jnp.bfloat16).astype(jnp.float32)
+    parts = jnp.where(place < LANES // 2, high, table - high).astype(jnp.bfloat16)
+    unit = (
+        lax.broadcasted_iota(jnp.int32, (rows, rows), 0)
+        == lax.broadcasted_iota(jnp.int32, (rows, rows), 1)
+    )
     depth = hid.shape[1]
-    tok[r, aligned(s, rows), depth : depth + LANES] = jnp.where(
-        lane < LANES // 2, high.astype(jnp.float32), low.astype(jnp.float32)
+    tok[r, aligned(s, rows), depth : depth + LANES] = lax.dot_general(
+        jnp.where(unit, 1.0, 0.0).astype(jnp.bfloat16),
+        parts,
+        (((1,), (1,)), ((), ())),
+        preferred_element_type=jnp.float32,
     ).astype(jnp.bfloat16)
 
     for t in range(2):
@@ -382,6 +390,7 @@
         kv2(t, 2, far, mate).wait_recv()
 
     wo_pass(0)
+    wo_pass(1)
     query_row = s * rows + lax.broadcasted_iota(jnp.int32, (rows, full), 0)
     allowed = lax.broadcasted_iota(jnp.int32, (rows, full), 1) <= query_row
 
@@ -405,7 +414,7 @@
 
         @pl.when(b == batch // 2)
         def _():
-            wo_pass(1)
+            wo_pass(2)
 
         return carry
 
@@ -435,11 +444,10 @@
         ).astype(jnp.bfloat16)
         pr(j, 2).start()
 
+    wo_pass(3)
     project(s)
-    wo_pass(2)
     wo_own(mate).wait_recv()
     project(mate)
-    wo_pass(3)
     pass_pair(s)
     pass_pair(mate)
     for c in range(chunks):
@@ -488,27 +496,36 @@
             piece(seq, role), piece(seq, role), tc_s.at[i, path], tc_r.at[i, path], {"seq": mate}
         )
 
-    def yc(i, path, role):
+    half = depth // 2
+
+    def yc(i, path, role, h):
         seq = far if path else mate
-        return remote(
-            y.at[role, aligned(seq, rows), :],
-            y_core.at[i, path],
-            yc_s.at[i, path],
-            yc_r.at[i, path],
+        block = pl.ds(h * half, half)
+        return remote(
+            y.at[role, aligned(seq, rows), block],
+            y_core.at[i, path, :, block],
+            yc_s.at[i, path * 2 + h],
+            yc_r.at[i, path * 2 + h],
             {"seq": mate},
         )
 
-    def yx(i, role):
-        return remote(
-            y.at[role, aligned(side, rows), :], y_x.at[i], yx_s.at[i], yx_r.at[i], {"seq": side}
-        )
-
-    def yz(kind):
-        return remote(
-            y.at[role_of((1, 3, 2)[kind]), aligned(s, rows), :],
-            y_role.at[kind],
-            yz_s.at[kind],
-            yz_r.at[kind],
+    def yx(i, role, h):
+        block = pl.ds(h * half, half)
+        return remote(
+            y.at[role, aligned(side, rows), block],
+            y_x.at[i, :, block],
+            yx_s.at[i, h],
+            yx_r.at[i, h],
+            {"seq": side},
+        )
+
+    def yz(kind, h):
+        block = pl.ds(h * half, half)
+        return remote(
+            y.at[role_of((1, 3, 2)[kind]), aligned(s, rows), block],
+            y_role.at[kind, :, block],
+            yz_s.at[kind, h],
+            yz_r.at[kind, h],
             to_role((1, 1, 2)[kind]),
         )
 
@@ -524,28 +541,31 @@
     step_f = hidden_width // 3 if hidden_width % 3 == 0 else hidden_width
     gate_lane = lax.broadcasted_iota(jnp.int32, (full, LANES), 1) % (LANES // 2)
 
-    def pass_core(i):
+    def pass_core(i, h):
         role = role_of(i)
-        yc(i, 0, role).wait_recv()
-        yc(i, 1, role).wait_recv()
+        block = pl.ds(h * half, half)
+        yc(i, 1, role, h).wait_recv()
         spot = aligned(side, rows)
-        y[role, spot, :] = (
-            y[role, spot, :].astype(jnp.float32) + y_core[i, 1].astype(jnp.float32)
+        y[role, spot, block] = (
+            y[role, spot, block].astype(jnp.float32) + y_core[i, 1, :, block].astype(jnp.float32)
         ).astype(jnp.bfloat16)
-        yx(i, role).start()
-
-    def summed(i):
+        yx(i, role, h).start()
+
+    def summed(i, h):
         role = role_of(i)
-        yx(i, role).wait_recv()
+        block = pl.ds(h * half, half)
+        yc(i, 0, role, h).wait_recv()
+        yx(i, role, h).wait_recv()
         return (
-            y[role, aligned(s, rows), :].astype(jnp.float32)
-            + y_core[i, 0].astype(jnp.float32)
-            + y_x[i].astype(jnp.float32)
-        )
-
-    def settle(i, kind):
-        y[role_of(i), aligned(s, rows), :] = summed(i).astype(jnp.bfloat16)
-        yz(kind).start()
+            y[role, aligned(s, rows), block].astype(jnp.float32)
+            + y_core[i, 0, :, block].astype(jnp.float32)
+            + y_x[i, :, block].astype(jnp.float32)
+        )
+
+    def settle(i, kind, h):
+        block = pl.ds(h * half, half)
+        y[role_of(i), aligned(s, rows), block] = summed(i, h).astype(jnp.bfloat16)
+        yz(kind, h).start()
 
     def one_block(i, carry):
         role = role_of(i)
@@ -578,31 +598,41 @@
             block = pl.ds(j * cols, cols)
             product = jnp.dot(act[...], dw[0, :, block], preferred_element_type=jnp.float32)
             y[role, :, block] = (product * share).astype(jnp.bfloat16)
-        yc(i, 1, role).start()
-        yc(i, 0, role).start()
+            if j % (seqs // 2) == seqs // 2 - 1:
+                yc(i, 1, role, j // (seqs // 2)).start()
+                yc(i, 0, role, j // (seqs // 2)).start()
 
         @pl.when(i > 1)
         def _():
-            pass_core(i - 1)
+            for h in range(2):
+                pass_core(i - 1, h)
 
         return carry
 
     lax.fori_loop(0, roles, one_block, 0)
-    pass_core(3)
-    pass_core(0)
-    settle(1, 0)
-    second = summed(2)
-    settle(3, 1)
-    yz(1).wait_recv()
-    y[role_of(2), aligned(s, rows), :] = (second + y_role[1].astype(jnp.float32)).astype(
-        jnp.bfloat16
-    )
-    yz(2).start()
-    total = hid[...] + summed(0)
-    for kind in (0, 2):
-        yz(kind).wait_recv()
-        total = total + y_role[kind].astype(jnp.float32)
-    out_ref[0] = total.astype(out_ref.dtype)
+    for h in range(2):
+        pass_core(3, h)
+    for h in range(2):
+        pass_core(0, h)
+    for h in range(2):
+        settle(1, 0, h)
+    for h in range(2):
+        settle(3, 1, h)
+    for h in range(2):
+        block = pl.ds(h * half, half)
+        second = summed(2, h)
+        yz(1, h).wait_recv()
+        y[role_of(2), aligned(s, rows), block] = (
+            second + y_role[1, :, block].astype(jnp.float32)
+        ).astype(jnp.bfloat16)
+        yz(2, h).start()
+    for h in range(2):
+        block = pl.ds(h * half, half)
+        total = hid[:, block] + summed(0, h)
+        for kind in (0, 2):
+            yz(kind, h).wait_recv()
+            total = total + y_role[kind, :, block].astype(jnp.float32)
+        out_ref[0, :, block] = total.astype(out_ref.dtype)
 
     for off in offs:
         for t in range(2):
@@ -611,7 +641,8 @@
         for j in range(seqs):
             pr(j, kind).wait_send()
         tz(kind, r, role_of(1)).wait_send()
-        yz(kind).wait_send()
+        for h in range(2):
+            yz(kind, h).wait_send()
         for t in range(2):
             kv2(t, kind, s, mate).wait_send()
     wo_own(s).wait_send()
@@ -622,10 +653,11 @@
             wo_mate(s, g, c, path).wait_send()
     for i in range(roles):
         tx(i, s, r).wait_send()
-        yx(i, r).wait_send()
         for path in range(2):
+            yx(i, r, path).wait_send()
             tc(i, path, s, r).wait_send()
-            yc(i, path, r).wait_send()
+            for h in range(2):
+                yc(i, path, r, h).wait_send()
 
 
 def fused(
@@ -648,6 +680,8 @@
     full = rows * seqs
     bf16, f32 = jnp.bfloat16, jnp.float32
     gain = norm_gain.reshape(1, depth)
+    route_experts = route_experts.transpose(0, 2, 1)
+    route_gates = route_gates.transpose(0, 2, 1)
     vmem = [
         pltpu.VMEM(query_rows.shape, bf16),
         pltpu.VMEM((2, batch, full, HEAD_WIDTH), bf16),
@@ -672,7 +706,8 @@
     ]
     dma = pltpu.SemaphoreType.DMA
     counts = [(2, roles)] * 2 + [(2, 3)] * 2 + [(9,)] * 2 + [(4,)] * 4 + [(seqs, 3)] * 2
-    counts += [(3,)] * 2 + [(roles,)] * 2 + [(roles, 2)] * 4 + [(roles,)] * 2 + [(3,)] * 2
+    counts += [(3,)] * 2 + [(roles,)] * 2 + [(roles, 2)] * 2 + [(roles, 4)] * 2
+    counts += [(roles, 2)] * 2 + [(3, 2)] * 2
     return pl.pallas_call(
         partial(layer_kernel, roles, seqs),
         out_shape=jax.ShapeDtypeStruct(residual.shape, bf16),

time: 120 us -> 116 us (0.967)
  local copies, waits for them, and re-layouts: 4.42 us -> 1.67 us
    unnamed x3 -> x1, local copies, waits for them, and re-layouts: 4.42 us -> 1.67 us
    pallas_call x1, Pallas kernels: 115 us -> 114 us  [fused(): pl.pallas_call(partial(layer_kernel, roles, seqs), out_shape=jax.ShapeDty...]
where the time goes in v3:
time: 116 us
  Pallas kernels  114 us (98%)
  local copies, waits for them, and re-layouts  1.67 us (1%)
    pallas_call x1, Pallas kernels, fused(): pl.pallas_call(partial(layer_kernel, roles, seqs), out_shape=jax.ShapeDty...  114 us

profile of v3, /device:TPU:0, one launch (start us, length us, event | category | flops | bytes accessed | tf_op | source)
XLA Modules:
  0.0 115.8 jit_solution(3356096752184117583)
XLA Ops:
  0.0 114.1 %shard_map.109 = bf16[1,64,2048]{2,1,0:T(8,128)(2,1)} custom-call(bf16[4,64,1024]{2,1,0:T(8,128)(2,1)} %q_hbm.1, bf16[4,16,512]{2,1,0:T(8,128)(2,1)} %k_hbm.1, bf16[4,16,512]{2,1,0:T(8,128)(2,1)} %v_hbm.1, bf16[1024,512]{1,0:T(8,128)(2,1)} %wo_hbm.1, bf16[1,64,2048]{2,1,0:T(8,128)(2,1)} %res_hbm.1, f32[1,2048]{1,0:T(1,128)} %bitcast.3, s32[1,8,64]{2,1,0:T(8,128)} %bitcast.4, ...), custom_call_target="tpu_custom_call" | custom-call | tf_op jit(solution)/shard_map/pallas_call | solution.py:711
  114.1 1.7 %copy.13 = bf16[1,64,2048]{2,1,0:T(8,128)(2,1)} copy(bf16[1,64,2048]{2,1,0:T(8,128)(2,1)} %shard_map.109) | data formatting | bytes 524288

commit v4 on v3

--- a/solution.py
+++ b/solution.py
@@ -586,6 +586,11 @@
         tc(i, 0, mate, role).wait_recv()
         tc(i, 1, far, role).wait_recv()
 
+        @pl.when(i > 1)
+        def _():
+            for h in range(2):
+                pass_core(i - 1, h)
+
         shares = tok[role, :, depth : depth + LANES].astype(jnp.float32)
         share = jnp.sum(jnp.where(gate_lane == expert, shares, 0.0), axis=1, keepdims=True)
         inputs = tok[role, :, 0:depth]
@@ -601,11 +606,6 @@
             if j % (seqs // 2) == seqs // 2 - 1:
                 yc(i, 1, role, j // (seqs // 2)).start()
                 yc(i, 0, role, j // (seqs // 2)).start()
-
-        @pl.when(i > 1)
-        def _():
-            for h in range(2):
-                pass_core(i - 1, h)
 
         return carry
 

time: 116 us -> 116 us (level)
  no operation moved by 1% of the time
where the time goes in v4:
time: 116 us; the launch traced here: 115 us
  Pallas kernels  114 us (98%)
  local copies, waits for them, and re-layouts  1.67 us (1%)
    pallas_call x1, Pallas kernels, fused(): pl.pallas_call(partial(layer_kernel, roles, seqs), out_shape=jax.ShapeDty...  114 us

profile of v4, /device:TPU:0, one launch (start us, length us, event | category | flops | bytes accessed | tf_op | source)
XLA Modules:
  0.0 115.5 jit_solution(7036059988638048983)
XLA Ops:
  0.0 113.8 %shard_map.109 = bf16[1,64,2048]{2,1,0:T(8,128)(2,1)} custom-call(bf16[4,64,1024]{2,1,0:T(8,128)(2,1)} %q_hbm.1, bf16[4,16,512]{2,1,0:T(8,128)(2,1)} %k_hbm.1, bf16[4,16,512]{2,1,0:T(8,128)(2,1)} %v_hbm.1, bf16[1024,512]{1,0:T(8,128)(2,1)} %wo_hbm.1, bf16[1,64,2048]{2,1,0:T(8,128)(2,1)} %res_hbm.1, f32[1,2048]{1,0:T(1,128)} %bitcast.3, s32[1,8,64]{2,1,0:T(8,128)} %bitcast.4, ...), custom_call_target="tpu_custom_call" | custom-call | tf_op jit(solution)/shard_map/pallas_call | solution.py:711
  113.8 1.7 %copy.13 = bf16[1,64,2048]{2,1,0:T(8,128)(2,1)} copy(bf16[1,64,2048]{2,1,0:T(8,128)(2,1)} %shard_map.109) | data formatting | bytes 524288
